TPU v7x, 32 devices: a whole 2x2x4 slice. The times are simulated.
32 devices in a mesh: ma: 8 (over z, y), sa: 4 (over x, core).
Axes of the slice: x: 2, y: 2, z: 4, core: 2. Of those that a mesh axis runs over, the one named last changes fastest.
Arguments:
- initial_heat_matrix: float32 [128, 128, 8192], P('ma', 'sa'), may hold values from -6 to 6
- conductivity: float32 [128, 8192], P('sa'), may hold values from 0.5 to 2
- laser_x: int32 [128, 2], P('ma'), may hold values from 0 to 127
- laser_y: int32 [128, 2], P('ma'), may hold values from 0 to 127
- pixel_cell: int32 [128, 512], P('sa', 'ma'), may hold values from 0 to 127, as said below
- observed: float32 [128, 512], P('sa', 'ma'), may hold values from -6 to 6
- obs_var: float32 [128, 512], P('sa', 'ma'), may hold values from 20 to 400
Outputs:
- analysis: float32 [128, 128, 8192], P('ma', 'sa')
Inputs may be any that keep to these rules, and one draw needn't show every extreme that they name: `pixel_cell`: pixel column j views a surface cell y of its own plane; y lies within 2 of j // 4 and in the same aligned group of 16 cells as that value.
All inputs are finite; a program needn't handle non-finite values.
Results may differ from a plain program's by a relative error of at most 0.000096.
Values sent between devices are 32-bit elements; how exact they have to be, the bound alone decides.
A program may use at most 384 MiB of HBM per device.

v0:
```python
import jax
import jax.numpy as jnp
from jax import lax
from jax.sharding import PartitionSpec as P

CELLS_DEPTHWISE = 64
step_dt = 0.025
alpha_cond = 0.05
laser_power = 12.0
beam_spot_width = 18.0


def extended(block, sides, width):
    for axis, dim in sides:
        count = lax.axis_size(axis)
        forward = [(i, i + 1) for i in range(count - 1)]
        backward = [(target, source) for source, target in forward]
        low = lax.ppermute(
            lax.slice_in_dim(block, block.shape[dim] - width, None, axis=dim), axis, forward
        )
        high = lax.ppermute(lax.slice_in_dim(block, 0, width, axis=dim), axis, backward)
        block = jnp.concatenate([low, block, high], axis=dim)
    return block


def conduct(field_ext, cond_ext, first_plane, spot_x, spot_y):
    kext = cond_ext[None] * (1.0 + alpha_cond * field_ext * field_ext)
    fpad = jnp.pad(field_ext, ((0, 0), (0, 0), (1, 1), (1, 1)))
    kpad = jnp.pad(kext, ((0, 0), (0, 0), (1, 1), (1, 1)))
    centre = fpad[:, 1:-1, 1:-1, 1:-1]
    kcentre = kpad[:, 1:-1, 1:-1, 1:-1]
    shifted = [
        (slice(2, None), slice(1, -1), slice(1, -1)),
        (slice(None, -2), slice(1, -1), slice(1, -1)),
        (slice(1, -1), slice(2, None), slice(1, -1)),
        (slice(1, -1), slice(None, -2), slice(1, -1)),
        (slice(1, -1), slice(1, -1), slice(2, None)),
        (slice(1, -1), slice(1, -1), slice(None, -2)),
    ]
    flux = jnp.zeros_like(centre)
    for pick in shifted:
        neighbour = fpad[(slice(None),) + pick]
        kneigh = kpad[(slice(None),) + pick]
        flux = flux + 0.5 * (kcentre + kneigh) * (neighbour - centre)
    width = centre.shape[1]
    rows_y = centre.shape[2]
    depth = centre.shape[3]
    xglob = first_plane + jnp.arange(width, dtype=jnp.int32)
    yglob = jnp.arange(rows_y, dtype=jnp.int32)
    delta_x = (xglob[None, :] - spot_x[:, None]).astype(jnp.float32)
    delta_y = (yglob[None, :] - spot_y[:, None]).astype(jnp.float32)
    spot = laser_power * jnp.exp(
        -(delta_x[:, :, None] ** 2 + delta_y[:, None, :] ** 2) / beam_spot_width
    )
    surface_top = (jnp.arange(depth, dtype=jnp.int32) == depth - 1).astype(jnp.float32)
    heat = spot[:, :, :, None] * surface_top[None, None, None, :]
    return centre + step_dt * (flux + heat)


def transform(block, mix):
    fmean = jnp.mean(block, axis=0)
    anom = block - fmean[None]
    return fmean[None] + jnp.einsum("jxc,jk->kxc", anom, mix, precision=lax.Precision.HIGHEST)


def lower_factor(amat):
    count = amat.shape[0]
    positions = jnp.arange(count, dtype=jnp.int32)

    def column_step(index_j, factor):
        row_j = lax.dynamic_slice_in_dim(factor, index_j, 1, 0)[0]
        row_j = jnp.where(positions < index_j, row_j, 0.0)
        column = lax.dynamic_slice_in_dim(amat, index_j, 1, 1)[:, 0]
        rest = column - jnp.dot(factor, row_j, precision=lax.Precision.HIGHEST)
        pivot = jnp.sqrt(lax.dynamic_slice_in_dim(rest, index_j, 1, 0)[0])
        fresh = jnp.where(
            positions > index_j, rest / pivot, jnp.where(positions == index_j, pivot, 0.0)
        )
        return jnp.where((positions == index_j)[None, :], fresh[:, None], factor)

    return lax.fori_loop(0, count, column_step, jnp.zeros_like(amat))


def lower_inverse(factor):
    count = factor.shape[0]
    positions = jnp.arange(count, dtype=jnp.int32)

    def row_step(index_i, inverse):
        row_i = lax.dynamic_slice_in_dim(factor, index_i, 1, 0)[0]
        pivot = lax.dynamic_slice_in_dim(row_i, index_i, 1, 0)[0]
        unit = (positions == index_i).astype(jnp.float32)
        fresh = (unit - jnp.dot(row_i, inverse, precision=lax.Precision.HIGHEST)) / pivot
        return jnp.where((positions == index_i)[:, None], fresh[None, :], inverse)

    return lax.fori_loop(0, count, row_step, jnp.zeros_like(factor))


def per_device(initial_heat_matrix, conductivity, laser_x, laser_y, pixel_cell, observed, obs_var):
    members, planes, columns = initial_heat_matrix.shape
    depth = CELLS_DEPTHWISE
    rows_y = columns // depth
    first = lax.axis_index("sa") * planes
    total_planes = planes * lax.axis_size("sa")
    field = initial_heat_matrix.reshape(members, planes, rows_y, depth)
    cond_grid = conductivity.reshape(1, planes, rows_y, depth)
    stacked = jnp.concatenate([field, cond_grid], axis=0)
    wider = extended(stacked, (("sa", 1),), 2)
    cond_wide = wider[members]
    middle = conduct(wider[:members], cond_wide, first - 1, laser_x[:, 0], laser_y[:, 0])
    plane_ids = first - 1 + jnp.arange(planes + 2, dtype=jnp.int32)
    inside = ((plane_ids >= 0) & (plane_ids < total_planes)).astype(jnp.float32)
    middle = middle * inside[None, :, None, None]
    field = conduct(middle, cond_wide[1:-1], first, laser_x[:, 1], laser_y[:, 1])
    member_states = field.reshape(members, planes, columns)
    gathered = lax.all_to_all(member_states, "ma", split_axis=2, concat_axis=0, tiled=True)
    total_members = gathered.shape[0]
    group_rows = gathered.shape[2] // depth
    surface = gathered.reshape(total_members, planes, group_rows, depth)[:, :, :, depth - 1]
    group_rows = surface.shape[2]
    local_rows = pixel_cell % group_rows
    onehot = (
        local_rows[:, None, :] == jnp.arange(group_rows, dtype=jnp.int32)[None, :, None]
    ).astype(jnp.float32)
    seen = jnp.einsum("kxy,xyj->kxj", surface, onehot, precision=lax.Precision.HIGHEST)
    seen_mean = jnp.mean(seen, axis=0)
    seen_anom = seen - seen_mean[None]
    innovation = observed - seen_mean
    weight = 1.0 / obs_var
    gram_part = jnp.einsum(
        "kxj,lxj->kl", seen_anom * weight[None], seen_anom, precision=lax.Precision.HIGHEST
    )
    proj_part = jnp.einsum(
        "kxj,xj->k", seen_anom, weight * innovation, precision=lax.Precision.HIGHEST
    )
    gram, proj = lax.psum((gram_part, proj_part), ("ma", "sa"))
    count = gram.shape[0]
    eye = jnp.eye(count, dtype=jnp.float32)
    amat = eye + gram / (count - 1)
    factor = lower_factor(amat)
    inverse = lower_inverse(factor)
    wroot = inverse.T
    middle_sol = jnp.dot(inverse, proj, precision=lax.Precision.HIGHEST)
    wmean = jnp.dot(wroot, middle_sol, precision=lax.Precision.HIGHEST) / (count - 1)
    mix = wroot + wmean[:, None]
    done = transform(gathered, mix)
    return lax.all_to_all(done, "ma", split_axis=0, concat_axis=2, tiled=True)


def solution(mesh):
    placed = (
        P("ma", "sa", None),
        P("sa", None),
        P("ma", None),
        P("ma", None),
        P("sa", "ma"),
        P("sa", "ma"),
        P("sa", "ma"),
    )
    return jax.shard_map(
        per_device, mesh=mesh, in_specs=placed, out_specs=P("ma", "sa", None), check_vma=False
    )
```

profile of v0, /device:TPU:0, one launch (start us, length us, event | category | flops | bytes accessed | tf_op | source)
XLA Modules:
  0.0 2191.7 jit_solution(17658031716975416276)
XLA Ops:
  6.5 27.0 %reshape.177 = f32[16,32,128,64]{3,2,1,0:T(8,128)} reshape(f32[16,32,8192]{2,1,0:T(8,128)} %param.11) | data formatting | bytes 33554432 | tf_op jit(solution)/shard_map/reshape | solution.py:104
  33.5 23.3 %constant_dynamic-update-slice_fusion.1 = f32[17,32,128,64]{3,2,1,0:T(8,128)} fusion(f32[16,32,128,64]{3,2,1,0:T(8,128)} %reshape.177), kind=kLoop, calls=%fused_computation.160 | loop fusion | bytes 50331648
  56.8 0.8 reshape.178
  57.7 1.5 constant_dynamic-update-slice_fusion
  59.1 4.1 fusion.104
  63.2 2.8 copy.15
  66.0 3.4 collective-permute-start
  69.4 1.7 copy.16
  71.1 1.5 collective-permute-start.1
  73.0 0.9 exponential_multiply_fusion.1
  74.0 1.8 copy.17
  75.8 1.4 collective-permute-done.1
  77.2 2.9 copy.18
  80.1 26.2 %pad_maximum_fusion = f32[17,36,128,64]{3,2,1,0:T(8,128)} fusion(f32[17,2,128,64]{3,2,1,0:T(8,128)} %copy.18, f32[17,32,128,64]{3,2,1,0:T(8,128)} %constant_dynamic-update-slice_fusion, f32[17,2,128,64]{3,2,1,0:T(8,128)S(1)} %copy.17), kind=kLoop, calls=%fused_computation.30 | loop fusion | flops 10027008 | bytes 40108032 | tf_op jit(solution)/shard_map/concatenate | solution.py:22
  106.3 3.5 maximum_bitcast_fusion
  109.8 3.2 maximum_bitcast_fusion.1
  113.0 36.7 %fusion.23 = (f32[16,36,128,64]{3,2,1,0:T(8,128)}, f32[16,36,128,64]{3,2,1,0:T(8,128)}) fusion(f32[36,128,64]{2,1,0:T(8,128)} %maximum_bitcast_fusion, f32[17,36,128,64]{3,2,1,0:T(8,128)} %pad_maximum_fusion), kind=kLoop, calls=%fused_computation.32 | loop fusion | flops 18874368 | bytes 57802752 | tf_op jit(solution)/shard_map/mul | solution.py:27
  149.7 179.5 %fusion.49 = (f32[16,34,128,64]{3,2,1,0:T(8,128)}, f32[16,34,128,64]{3,2,1,0:T(8,128)}) fusion(f32[34,128,64]{2,1,0:T(8,128)} %maximum_bitcast_fusion.1, f32[34]{0:T(128)S(1)} %and_convert_fusion, f32[64]{0:T(128)S(1)} %compare_convert_fusion, f32[16,34,128]{2,1,0:T(8,128)S(1)} %exponential_multiply_fusion, f32[16,36,128,64]{3,2,1,0:T(8,128)} %get-tuple-element.281, ...), kind=kLoop, calls=%fused_computation.66 | loop fusion | flops 178257920 | bytes 295256448 | tf_op jit(solution)/shard_map/mul | solution.py:27
  329.2 165.0 %fusion.66 = f32[16,32,128,64]{3,2,1,0:T(8,128)} fusion(f32[16,34,128,64]{3,2,1,0:T(8,128)} %get-tuple-element.278, f32[16,34,128,64]{3,2,1,0:T(8,128)} %get-tuple-element.279, f32[64]{0:T(128)S(1)} %compare_convert_fusion, f32[16,32,128]{2,1,0:T(8,128)S(1)} %copy-done.4), kind=kLoop, calls=%fused_computation.95 | loop fusion | flops 138412032 | bytes 289669376 | tf_op jit(solution)/shard_map/add | solution.py:57
  494.2 45.2 %copy.30 = f32[16,32,128,64]{1,0,3,2:T(8,128)} copy(f32[16,32,128,64]{3,2,1,0:T(8,128)} %fusion.66) | data formatting | bytes 33554432 | tf_op jit(solution)/shard_map/reshape | solution.py:114
  539.4 67.4 %reshape.193 = f32[8,1,524288]{2,1,0:T(1,128)} reshape(f32[8192,16,32]{2,1,0:T(8,128)} %bitcast.86) | data formatting | bytes 33554432
  606.7 6.0 all-to-all-start
  612.8 353.2 %all-to-all-done = f32[8,1,524288]{2,1,0:T(1,128)} async-done(((f32[8,1,524288]{2,1,0:T(1,128)}), f32[8,1,524288]{2,1,0:T(1,128)}, u32[]{:S(2)}, u32[]{:S(2)}) %all-to-all-start) | async-done | bytes 16777248 | tf_op jit(solution)/shard_map/all_to_all | solution.py:115
  966.6 50.5 %reduce.1 = f32[8,524288]{1,0:T(8,128)} reduce(f32[8,1,524288]{2,1,0:T(1,128)} %all-to-all-done, f32[]{:T(128)} %broadcast.207), dimensions={1}, to_apply=%all_to_all.26.reduce_sub_computation | reduce | bytes 33554436 | tf_op jit(solution)/shard_map/all_to_all | solution.py:115
  1017.1 55.4 %reshape.194 = f32[8192,16,32]{2,1,0:T(8,128)} reshape(f32[8,524288]{1,0:T(8,128)} %reduce.1) | data formatting | bytes 33554432
  1072.5 42.5 %copy.23 = f32[8,16,32,1024]{3,2,1,0:T(8,128)} copy(f32[8,16,32,1024]{2,1,3,0:T(8,128)} %bitcast.9) | data formatting | bytes 33554432 | tf_op jit(solution)/shard_map/all_to_all | solution.py:115
  1114.9 44.4 %copy.26 = f32[8,16,32,1024]{3,1,0,2:T(8,128)} copy(f32[8,16,32,1024]{2,1,3,0:T(8,128)} %bitcast.9) | data formatting | bytes 33554432 | tf_op jit(solution)/shard_map/all_to_all | solution.py:115
  1159.3 25.8 %reshape.180 = f32[128,32,16,64]{3,2,1,0:T(8,128)} reshape(f32[8,16,32,1024]{3,2,1,0:T(8,128)} %copy.23) | data formatting | bytes 33554432 | tf_op jit(solution)/shard_map/reshape | solution.py:118
  1185.1 25.2 %slice.190 = f32[128,32,16,1]{3,2,1,0:T(8,128)} slice(f32[128,32,16,64]{3,2,1,0:T(8,128)} %reshape.180), slice={[0:128], [0:32], [0:16], [63:64]} | slice | bytes 524288 | tf_op jit(solution)/shard_map/slice | solution.py:118
  1210.3 19.1 copy.34
  1229.4 1.2 fusion.105
  1230.6 3.3 fusion.87
  1233.9 34.8 %copy.31 = f32[16,32,8,1024]{3,2,1,0:T(8,128)} copy(f32[16,32,8,1024]{1,0,3,2:T(8,128)} %bitcast.7) | data formatting | bytes 33554432 | tf_op jit(solution)/shard_map/all_to_all | solution.py:115
  1268.7 7.9 bitcast_reduce_fusion
  1276.7 12.3 bitcast_subtract_fusion
  1289.0 0.8 convolution_bitcast_fusion.3
  1289.8 48.9 %psum.15 = f32[128]{0:T(128)S(1)} all-reduce(f32[128]{0:T(128)S(1)} %convolution_bitcast_fusion.3), channel_id=1, replica_groups=mesh['ma'=8,'sa'=4] {'ma','sa'}, use_global_device_ids=true, to_apply=%region_7.8 | all-reduce | flops 128 | bytes 1024 | tf_op jit(solution)/shard_map/psum | solution.py:135
  1338.7 24.4 %all-reduce.6.cloned.1.call-done = f32[128,128]{1,0:T(8,128)} async-done(((f32[128,128]{1,0:T(8,128)}), f32[128,128]{1,0:T(8,128)}) %all-reduce.6.cloned.1.call-update) | async-done | bytes 65552 | tf_op jit(solution)/shard_map/psum | solution.py:135
  1363.1 0.9 multiply_add_fusion
  1364.0 212.1 %while.33 = (s32[]{:T(128)}, f32[128,128]{1,0:T(8,128)S(1)}, f32[128,128]{0,1:T(8,128)S(1)}, s32[]{:T(128)}, s32[]{:T(128)}) while((s32[]{:T(128)}, f32[128,128]{1,0:T(8,128)S(1)}, f32[128,128]{0,1:T(8,128)S(1)}, s32[]{:T(128)}, s32[]{:T(128)}) %tuple.94), condition=%wide.region_4.5_spmd.clone.clone, body=%wide.region_3.4_spmd.clone.clone.sunk | while | flops 246915 | bytes 332648 | solution.py:81
  1576.2 195.6 %while.32 = (s32[]{:T(128)}, f32[128,128]{1,0:T(8,128)S(1)}, f32[128,128]{1,0:T(8,128)S(1)}, s32[]{:T(128)}, s32[]{:T(128)}, /*index=5*/s32[]{:T(128)}) while((s32[]{:T(128)}, f32[128,128]{1,0:T(8,128)S(1)}, f32[128,128]{1,0:T(8,128)S(1)}, s32[]{:T(128)}, s32[]{:T(128)}, /*index=5*/s32[]{:T(128)}) %tuple.93), condition=%wide.region_6.7_spmd.clone, body=%wide.region_5.6_spmd.clone.sunk | while | flops 246404 | bytes 200048 | solution.py:95
  1578.3 0.8 fusion.119
  1584.5 0.8 fusion.119
  1589.0 0.8 fusion.119
  1772.2 21.8 convolution_add_fusion
  1794.0 15.7 copy.27
  1809.6 368.8 %all_to_all.36 = f32[128,32,1024]{2,1,0:T(8,128)S(1)} all-to-all(f32[128,32,1024]{2,1,0:T(8,128)S(1)} %copy.27), channel_id=1, replica_groups=mesh['ma'=8,'sa'=4] {'ma'}, dimensions={0} | all-to-all | bytes 33554432 | tf_op jit(solution)/shard_map/all_to_all | solution.py:146
  2178.5 6.2 copy.35
  (1319 shorter events, 307.7 us)
Async XLA Ops:
  33.5 23.3 %copy-start.3 = (f32[32,8192]{1,0:T(8,128)S(1)}, f32[32,8192]{1,0:T(8,128)}, u32[]{:S(2)}) copy-start(f32[32,8192]{1,0:T(8,128)} %param.12) | copy-start | bytes 3145732
  33.5 39.2 %copy-start.8 = (s32[16,2]{0,1:T(2,128)S(1)}, s32[16,2]{0,1:T(2,128)}, u32[]{:S(2)}) copy-start(s32[16,2]{0,1:T(2,128)} %param.13) | copy-start | bytes 388
  33.5 39.3 %copy-start.9 = (s32[16,2]{0,1:T(2,128)S(1)}, s32[16,2]{0,1:T(2,128)}, u32[]{:S(2)}) copy-start(s32[16,2]{0,1:T(2,128)} %param.14) | copy-start | bytes 388
  66.0 8.0 collective-permute-start
  71.1 6.1 collective-permute-start.1
  106.3 3.5 copy-start
  149.7 179.5 %copy-start.4 = (f32[16,32,128]{2,1,0:T(8,128)S(1)}, f32[16,32,128]{2,1,0:T(8,128)}, u32[]{:S(2)}) copy-start(f32[16,32,128]{2,1,0:T(8,128)} %exponential_multiply_fusion.1) | copy-start | bytes 786436
  606.7 6.0 copy-start.5
  606.7 359.3 %all-to-all-start = ((f32[8,1,524288]{2,1,0:T(1,128)}), f32[8,1,524288]{2,1,0:T(1,128)}, u32[]{:S(2)}, u32[]{:S(2)}) async-start(f32[8,1,524288]{2,1,0:T(1,128)} %reshape.193), calls=%async_computation | async-start | bytes 33554432 | tf_op jit(solution)/shard_map/all_to_all | solution.py:115
  612.7 750.4 %all-reduce.6.cloned.1.call-start = ((), (), s32[]{:S(2)}) async-start(), calls=%async_computation.2 | async-start | bytes 131072 | tf_op jit(solution)/shard_map/psum | solution.py:135
  1210.3 20.3 copy-start.6
  1210.3 20.3 copy-start.7
  1268.7 95.3 %copy-start.2 = (f32[128,128]{1,0:T(8,128)S(1)}, f32[128,128]{1,0:T(8,128)}, u32[]{:S(2)}) copy-start(f32[128,128]{1,0:T(8,128)} %custom-call.1) | copy-start | bytes 196612
  1268.7 307.5 %copy-start.1 = (f32[128,128]{1,0:T(8,128)S(1)}, f32[128,128]{1,0:T(8,128)}, u32[]{:S(2)}) copy-start(f32[128,128]{1,0:T(8,128)} %custom-call) | copy-start | bytes 196612
Sparse Core Ops, SparseCore 0:
  1234.1 128.9 all-reduce.5
where the time goes:
time: 2200 us; the launch traced here: 2190 us
  local copies, waits for them, and re-layouts  605 us (28%)
  other arithmetic  514 us (23%)
  blocking collectives  418 us (19%)
  waiting for transfers between devices  379 us (17%)
  matrix products  152 us (7%)
  loops' own time  99.2 us (5%)
    all_to_all x1, blocking collectives, per_device(): return lax.all_to_all(done, 'ma', split_axis=0, concat_axis=2, tiled=True)  369 us
    all_to_all x1, waiting for transfers between devices, per_device(): lax.all_to_all(member_states, 'ma', split_axis=2, concat_axis=0, tiled=True)  353 us
    mul x4, other arithmetic, conduct(): kext = cond_ext[None] * (1.0 + alpha_cond * field_ext * field_ext)  223 us
    unnamed x25, local copies, waits for them, and re-layouts  165 us
    add x1, other arithmetic, conduct(): return centre + step_dt * (flux + heat)  165 us
    all_to_all x4, local copies, waits for them, and re-layouts, per_device(): lax.all_to_all(member_states, 'ma', split_axis=2, concat_axis=0, tiled=True)  122 us
    dot_general x128, matrix products, row_step(): jnp.dot(row_i, inverse, precision=lax.Precision.HIGHEST)  102 us
    another operation x1, loops' own time, lower_factor(): return lax.fori_loop(0, count, column_step, jnp.zeros_like(amat))  94.8 us
  transfers between devices with their start and end apart: 4, of which 3 were waited for; matrix products, arithmetic and copies ran while one was open for 3% of the time, Pallas kernels for 0%

commit v1 on v0

--- a/solution.py
+++ b/solution.py
@@ -112,7 +112,9 @@
     middle = middle * inside[None, :, None, None]
     field = conduct(middle, cond_wide[1:-1], first, laser_x[:, 1], laser_y[:, 1])
     member_states = field.reshape(members, planes, columns)
-    gathered = lax.all_to_all(member_states, "ma", split_axis=2, concat_axis=0, tiled=True)
+    pieces = jnp.split(member_states, lax.axis_size("ma"), axis=2)
+    received = lax.all_to_all(jnp.stack(pieces), "ma", 0, 0)
+    gathered = jnp.concatenate(received, axis=0)
     total_members = gathered.shape[0]
     group_rows = gathered.shape[2] // depth
     surface = gathered.reshape(total_members, planes, group_rows, depth)[:, :, :, depth - 1]

time: 2200 us -> 1930 us (0.88)
  local copies, waits for them, and re-layouts: 605 us -> 384 us
  other arithmetic: 514 us -> 459 us
  waiting for transfers between devices: 379 us -> 404 us
    all_to_all x4 -> x1, local copies, waits for them, and re-layouts: 122 us -> 15.2 us  [per_device(): received = lax.all_to_all(jnp.stack(pieces), 'ma', 0, 0)]
    unnamed x25 -> x26, local copies, waits for them, and re-layouts: 165 us -> 64.7 us
    all_to_all x1 -> x0, other arithmetic: 50.5 us -> none  [per_device(): lax.all_to_all(member_states, 'ma', split_axis=2, concat_axis=0, tiled=True)]
    another operation x0 -> x2, local copies, waits for them, and re-layouts: none -> 29.1 us  [the longest x1 26 us: per_device(): gathered.reshape(total_members, planes, group_rows, depth)]
    reshape x1 -> x0, local copies, waits for them, and re-layouts: 25.8 us -> none  [per_device(): gathered.reshape(total_members, planes, group_rows, depth)]
    psum x1, waiting for transfers between devices: 24.4 us -> 49.4 us  [per_device(): gram, proj = lax.psum((gram_part, proj_part), ('ma', 'sa'))]
  transfers between devices with their start and end apart: 4 -> 4, of which waited for: 3 -> 3; matrix products, arithmetic and copies ran while one was open for 3% -> 2% of each run, Pallas kernels for 0% -> 0%
where the time goes in v1:
time: 1930 us; the launch traced here: 1920 us
  other arithmetic  459 us (24%)
  blocking collectives  418 us (22%)
  waiting for transfers between devices  404 us (21%)
  local copies, waits for them, and re-layouts  384 us (20%)
  matrix products  141 us (7%)
  loops' own time  88.3 us (5%)
    all_to_all x1, blocking collectives, per_device(): return lax.all_to_all(done, 'ma', split_axis=0, concat_axis=2, tiled=True)  369 us
    all_to_all x1, waiting for transfers between devices, per_device(): received = lax.all_to_all(jnp.stack(pieces), 'ma', 0, 0)  353 us
    mul x4, other arithmetic, conduct(): kext = cond_ext[None] * (1.0 + alpha_cond * field_ext * field_ext)  223 us
    add x1, other arithmetic, conduct(): return centre + step_dt * (flux + heat)  165 us
    dot_general x128, matrix products, row_step(): jnp.dot(row_i, inverse, precision=lax.Precision.HIGHEST)  91.4 us
    another operation x1, loops' own time, lower_factor(): return lax.fori_loop(0, count, column_step, jnp.zeros_like(amat))  83.9 us
    dynamic_slice x128, local copies, waits for them, and re-layouts, column_step(): pivot = jnp.sqrt(lax.dynamic_slice_in_dim(rest, index_j, 1, 0)[0])  81.8 us
    dynamic_slice x128, local copies, waits for them, and re-layouts, row_step(): pivot = lax.dynamic_slice_in_dim(row_i, index_i, 1, 0)[0]  75.7 us
  transfers between devices with their start and end apart: 4, of which 3 were waited for; matrix products, arithmetic and copies ran while one was open for 2% of the time, Pallas kernels for 0%

profile of v1, /device:TPU:0, one launch (start us, length us, event | category | flops | bytes accessed | tf_op | source)
XLA Modules:
  0.0 1918.1 jit_solution(215052254243528551)
XLA Ops:
  6.5 27.0 %reshape.176 = f32[16,32,128,64]{3,2,1,0:T(8,128)} reshape(f32[16,32,8192]{2,1,0:T(8,128)} %param.11) | data formatting | bytes 33554432 | tf_op jit(solution)/shard_map/reshape | solution.py:104
  33.6 23.3 %constant_dynamic-update-slice_fusion.1 = f32[17,32,128,64]{3,2,1,0:T(8,128)} fusion(f32[16,32,128,64]{3,2,1,0:T(8,128)} %reshape.176), kind=kLoop, calls=%fused_computation.167 | loop fusion | bytes 50331648
  56.9 0.8 reshape.177
  57.7 1.5 constant_dynamic-update-slice_fusion
  59.2 4.1 fusion.112
  63.2 2.8 copy.22
  66.0 3.4 collective-permute-start
  69.4 1.7 copy.23
  71.1 1.8 collective-permute-start.1
  73.2 0.8 exponential_multiply_fusion.1
  74.2 1.8 copy.24
  76.1 1.1 collective-permute-done.1
  77.2 2.8 copy.25
  80.0 26.2 %pad_maximum_fusion = f32[17,36,128,64]{3,2,1,0:T(8,128)} fusion(f32[17,2,128,64]{3,2,1,0:T(8,128)} %copy.25, f32[17,32,128,64]{3,2,1,0:T(8,128)} %constant_dynamic-update-slice_fusion, f32[17,2,128,64]{3,2,1,0:T(8,128)S(1)} %copy.24), kind=kLoop, calls=%fused_computation.30 | loop fusion | flops 10027008 | bytes 40108032 | tf_op jit(solution)/shard_map/concatenate | solution.py:22
  106.2 3.5 maximum_bitcast_fusion
  109.6 3.2 maximum_bitcast_fusion.1
  112.9 36.7 %fusion.23 = (f32[16,36,128,64]{3,2,1,0:T(8,128)}, f32[16,36,128,64]{3,2,1,0:T(8,128)}) fusion(f32[36,128,64]{2,1,0:T(8,128)} %maximum_bitcast_fusion, f32[17,36,128,64]{3,2,1,0:T(8,128)} %pad_maximum_fusion), kind=kLoop, calls=%fused_computation.32 | loop fusion | flops 18874368 | bytes 57802752 | tf_op jit(solution)/shard_map/mul | solution.py:27
  149.6 179.5 %fusion.49 = (f32[16,34,128,64]{3,2,1,0:T(8,128)}, f32[16,34,128,64]{3,2,1,0:T(8,128)}) fusion(f32[34,128,64]{2,1,0:T(8,128)} %maximum_bitcast_fusion.1, f32[34]{0:T(128)S(1)} %and_convert_fusion, f32[64]{0:T(128)S(1)} %compare_convert_fusion, f32[16,34,128]{2,1,0:T(8,128)S(1)} %exponential_multiply_fusion, f32[16,36,128,64]{3,2,1,0:T(8,128)} %get-tuple-element.281, ...), kind=kLoop, calls=%fused_computation.66 | loop fusion | flops 178257920 | bytes 295256448 | tf_op jit(solution)/shard_map/mul | solution.py:27
  329.0 165.1 %fusion.66 = f32[16,32,128,64]{3,2,1,0:T(8,128)} fusion(f32[16,34,128,64]{3,2,1,0:T(8,128)} %get-tuple-element.278, f32[16,34,128,64]{3,2,1,0:T(8,128)} %get-tuple-element.279, f32[64]{0:T(128)S(1)} %compare_convert_fusion, f32[16,32,128]{2,1,0:T(8,128)S(1)} %copy-done.2), kind=kLoop, calls=%fused_computation.95 | loop fusion | flops 138412032 | bytes 289669376 | tf_op jit(solution)/shard_map/add | solution.py:57
  494.2 27.9 %reshape.178 = f32[16,32,8192]{2,1,0:T(8,128)} reshape(f32[16,32,128,64]{3,2,1,0:T(8,128)} %fusion.66) | data formatting | bytes 33554432 | tf_op jit(solution)/shard_map/reshape | solution.py:114
  522.1 3.2 fusion.92
  525.3 3.1 fusion.91
  528.4 3.2 fusion.90
  531.6 3.2 fusion.89
  534.8 3.2 fusion.88
  538.0 3.2 fusion.87
  541.1 3.2 fusion.86
  544.3 3.1 fusion.85
  547.4 5.8 all-to-all-start
  553.4 353.2 %all-to-all-done = f32[8,16,32,1024]{3,2,1,0:T(8,128)} async-done(((f32[8,16,32,1024]{3,2,1,0:T(8,128)}), f32[8,16,32,1024]{3,2,1,0:T(8,128)}, u32[]{:S(2)}, u32[]{:S(2)}) %all-to-all-start) | async-done | bytes 16777248 | tf_op jit(solution)/shard_map/all_to_all | solution.py:116
  906.6 26.0 %reshape_reshape.3 = f32[128,32,16,64]{3,2,1,0:T(8,128)} reshape(f32[8,16,32,1024]{3,2,1,0:T(8,128)} %all-to-all-done) | data formatting | bytes 33554432 | tf_op jit(solution)/shard_map/reshape;reshape | solution.py:120
  932.6 25.2 %slice.190 = f32[128,32,16,1]{3,2,1,0:T(8,128)} slice(f32[128,32,16,64]{3,2,1,0:T(8,128)} %reshape_reshape.3), slice={[0:128], [0:32], [0:16], [63:64]} | slice | bytes 524288 | tf_op jit(solution)/shard_map/slice | solution.py:120
  957.7 19.1 copy.34
  976.8 1.2 fusion.113
  978.0 3.3 fusion.95
  981.4 6.7 reduce_sum.18
  988.1 15.2 copy.30
  1003.3 8.6 bitcast_subtract_fusion
  1011.9 0.8 convolution_bitcast_fusion.3
  1012.7 48.8 %psum.15 = f32[128]{0:T(128)S(1)} all-reduce(f32[128]{0:T(128)S(1)} %convolution_bitcast_fusion.3), channel_id=1, replica_groups=mesh['ma'=8,'sa'=4] {'ma','sa'}, use_global_device_ids=true, to_apply=%region_7.8 | all-reduce | flops 128 | bytes 1024 | tf_op jit(solution)/shard_map/psum | solution.py:137
  1061.5 49.4 %all-reduce.6.cloned.1.call-done = f32[128,128]{1,0:T(8,128)} async-done(((f32[128,128]{1,0:T(8,128)}), f32[128,128]{1,0:T(8,128)}) %all-reduce.6.cloned.1.call-update) | async-done | bytes 65552 | tf_op jit(solution)/shard_map/psum | solution.py:137
  1110.9 0.9 multiply_add_fusion
  1111.8 201.6 %while.33 = (s32[]{:T(128)}, f32[128,128]{1,0:T(8,128)S(1)}, f32[128,128]{0,1:T(8,128)S(1)}, s32[]{:T(128)}, s32[]{:T(128)}) while((s32[]{:T(128)}, f32[128,128]{1,0:T(8,128)S(1)}, f32[128,128]{0,1:T(8,128)S(1)}, s32[]{:T(128)}, s32[]{:T(128)}) %tuple.85), condition=%wide.region_4.5_spmd.clone.clone, body=%wide.region_3.4_spmd.clone.clone.sunk | while | flops 246915 | bytes 332648 | solution.py:81
  1313.4 185.0 %while.32 = (s32[]{:T(128)}, f32[128,128]{1,0:T(8,128)S(1)}, f32[128,128]{1,0:T(8,128)S(1)}, s32[]{:T(128)}, s32[]{:T(128)}, /*index=5*/s32[]{:T(128)}) while((s32[]{:T(128)}, f32[128,128]{1,0:T(8,128)S(1)}, f32[128,128]{1,0:T(8,128)S(1)}, s32[]{:T(128)}, s32[]{:T(128)}, /*index=5*/s32[]{:T(128)}) %tuple.88), condition=%wide.region_6.7_spmd.clone, body=%wide.region_5.6_spmd.clone.sunk | while | flops 246404 | bytes 200048 | solution.py:95
  1498.8 21.7 %convolution_add_fusion = f32[128,32,1024]{2,0,1:T(8,128)} fusion(f32[128,32,1024]{2,0,1:T(8,128)} %bitcast_subtract_fusion, f32[32,1024]{1,0:T(8,128)S(1)} %broadcast_multiply_fusion, f32[128,128]{1,0:T(8,128)S(1)} %get-tuple-element.215, f32[128]{0:T(128)S(1)} %fusion.98), kind=kOutput, calls=%fused_computation.119 | convolution fusion | flops 6446661632 | bytes 33751552 | tf_op jit(solution)/shard_map/jxc,jk->kxc/dot_general | solution.py:63
  1520.5 15.5 copy.31
  1536.0 368.8 %all_to_all.23 = f32[128,32,1024]{2,1,0:T(8,128)S(1)} all-to-all(f32[128,32,1024]{2,1,0:T(8,128)S(1)} %copy.31), channel_id=1, replica_groups=mesh['ma'=8,'sa'=4] {'ma'}, dimensions={0} | all-to-all | bytes 33554432 | tf_op jit(solution)/shard_map/all_to_all | solution.py:148
  1904.8 6.2 copy.35
  (1317 shorter events, 299.4 us)
Async XLA Ops:
  33.6 23.3 %copy-start.1 = (f32[32,8192]{1,0:T(8,128)S(1)}, f32[32,8192]{1,0:T(8,128)}, u32[]{:S(2)}) copy-start(f32[32,8192]{1,0:T(8,128)} %param.12) | copy-start | bytes 3145732
  33.6 39.4 %copy-start.6 = (s32[16,2]{0,1:T(2,128)S(1)}, s32[16,2]{0,1:T(2,128)}, u32[]{:S(2)}) copy-start(s32[16,2]{0,1:T(2,128)} %param.13) | copy-start | bytes 388
  33.6 39.5 %copy-start.7 = (s32[16,2]{0,1:T(2,128)S(1)}, s32[16,2]{0,1:T(2,128)}, u32[]{:S(2)}) copy-start(s32[16,2]{0,1:T(2,128)} %param.14) | copy-start | bytes 388
  66.0 8.2 collective-permute-start
  71.1 6.1 collective-permute-start.1
  106.2 3.5 copy-start
  149.6 179.5 %copy-start.2 = (f32[16,32,128]{2,1,0:T(8,128)S(1)}, f32[16,32,128]{2,1,0:T(8,128)}, u32[]{:S(2)}) copy-start(f32[16,32,128]{2,1,0:T(8,128)} %exponential_multiply_fusion.1) | copy-start | bytes 786436
  522.1 31.3 %copy-start.3 = (s32[32,64]{1,0:T(8,128)S(1)}, s32[32,64]{1,0:T(8,128)}, u32[]{:S(2)}) copy-start(s32[32,64]{1,0:T(8,128)} %param.15) | copy-start | bytes 24580
  547.4 359.2 %all-to-all-start = ((f32[8,16,32,1024]{3,2,1,0:T(8,128)}), f32[8,16,32,1024]{3,2,1,0:T(8,128)}, u32[]{:S(2)}, u32[]{:S(2)}) async-start(f32[8,16,32,1024]{3,2,1,0:T(8,128)} %fusion.85), calls=%async_computation | async-start | bytes 33554432 | tf_op jit(solution)/shard_map/all_to_all | solution.py:116
  553.3 557.6 %all-reduce.6.cloned.1.call-start = ((), (), s32[]{:S(2)}) async-start(), calls=%async_computation.2 | async-start | bytes 131072 | tf_op jit(solution)/shard_map/psum | solution.py:137
  957.7 20.3 %copy-start.4 = (f32[32,64]{1,0:T(8,128)S(1)}, f32[32,64]{1,0:T(8,128)}, u32[]{:S(2)}) copy-start(f32[32,64]{1,0:T(8,128)} %param.16) | copy-start | bytes 24580
  957.7 20.3 %copy-start.5 = (f32[32,64]{1,0:T(8,128)S(1)}, f32[32,64]{1,0:T(8,128)}, u32[]{:S(2)}) copy-start(f32[32,64]{1,0:T(8,128)} %param.17) | copy-start | bytes 24580
Sparse Core Ops, SparseCore 0:
  981.5 129.2 all-reduce.5
